TPU v7x, 32 devices: a whole 2x2x4 slice. The times are simulated.
32 devices in a mesh: row: 8 (over z, y), col: 4 (over x, core).
Axes of the slice: x: 2, y: 2, z: 4, core: 2. Of those that a mesh axis runs over, the one named last changes fastest.
Arguments:
- layer_input: bfloat16 [1024, 12288], P(None, 'row'), may hold values from -6 to 6
- hidden_pre: bfloat16 [1024, 24576], P(None, 'col'), may hold values from -6 to 6
- out_grad: bfloat16 [1024, 12288], P(None, 'row'), may hold values from -8 to 8
- w_up: bfloat16 [12288, 24576], P('row', 'col'), may hold values from -0.0546875 to 0.0546875
- w_down: bfloat16 [24576, 12288], P('col', 'row'), may hold values from -0.0390625 to 0.0390625
Outputs:
- in_grad: bfloat16 [1024, 12288], P('col', 'row')
- up_grad: bfloat16 [12288, 24576], P('row', 'col')
- down_grad: bfloat16 [24576, 12288], P('col', 'row')
All inputs are finite; a program needn't handle non-finite values.
Results may differ from a plain program's by a relative error of at most 0.0051.
Values may be sent and summed in bfloat16 or wider, within the bound.
A program may use at most 320 MiB of HBM per device.

v0:
```python
import math
import jax
import jax.numpy as jnp
from jax import lax
from jax.sharding import PartitionSpec as P

GELU_COEF = 0.7978845608
CUBIC_COEF = 0.044715
CONTRACT_LAST = (((1,), (1,)), ((), ()))
CONTRACT_FIRST = (((0,), (0,)), ((), ()))


def gelu_value(pre_act):
    inner = GELU_COEF * (pre_act + CUBIC_COEF * pre_act * pre_act * pre_act)
    return 0.5 * pre_act * (1.0 + jnp.tanh(inner))


def gelu_slope(pre_act):
    inner = GELU_COEF * (pre_act + CUBIC_COEF * pre_act * pre_act * pre_act)
    tangent = jnp.tanh(inner)
    return 0.5 * (1.0 + tangent) + 0.5 * pre_act * (1.0 - tangent * tangent) * GELU_COEF * (
        1.0 + 3.0 * CUBIC_COEF * pre_act * pre_act
    )


def body(layer_input, hidden_pre, out_grad, w_up, w_down):
    token_count = out_grad.shape[0]
    scaling = 1.0 / math.sqrt(token_count)
    pre_act = hidden_pre.astype(jnp.float32)
    activated = gelu_value(pre_act).astype(jnp.bfloat16)
    down_total = lax.dot_general(
        activated, out_grad, CONTRACT_FIRST, preferred_element_type=jnp.float32
    )
    down_grad = (down_total * scaling).astype(jnp.bfloat16)
    local_sum = lax.dot_general(out_grad, w_down, CONTRACT_LAST, preferred_element_type=jnp.float32)
    summed = lax.psum(local_sum, "row")
    hidden_grad = (summed * gelu_slope(pre_act)).astype(jnp.bfloat16)
    up_total = lax.dot_general(
        layer_input, hidden_grad, CONTRACT_FIRST, preferred_element_type=jnp.float32
    )
    in_partial = lax.dot_general(
        hidden_grad, w_up, CONTRACT_LAST, preferred_element_type=jnp.float32
    )
    up_grad = (up_total * scaling).astype(jnp.bfloat16)
    in_grad = lax.psum_scatter(in_partial, "col", scatter_dimension=0, tiled=True).astype(
        jnp.bfloat16
    )
    return (in_grad, up_grad, down_grad)


def solution(mesh):
    placed = (P(None, "row"), P(None, "col"), P(None, "row"), P("row", "col"), P("col", "row"))
    return jax.shard_map(
        body,
        mesh=mesh,
        in_specs=placed,
        out_specs=(P("col", "row"), P("row", "col"), P("col", "row")),
        check_vma=False,
    )
```

profile of v0, /device:TPU:0, one launch (start us, length us, event | category | flops | bytes accessed | tf_op | source)
XLA Modules:
  0.0 922.6 jit_solution(7426446463446432995)
XLA Ops:
  7.2 0.0 copy-start
  7.2 0.0 all-reduce.2.cloned.1.call-start
  7.2 1.8 copy-done
  9.1 25.3 %fusion.21 = f32[1024,6144]{1,0:T(8,128)} fusion(bf16[1024,1536]{1,0:T(8,128)(2,1)S(1)} %copy-done, bf16[6144,1536]{1,0:T(8,128)(2,1)} %param.9), kind=kOutput, calls=%fused_computation.29 | convolution fusion | flops 19327352832 | bytes 47185920 | tf_op jit(solution)/shard_map/dot_general | solution.py:35
  34.4 0.0 all-reduce.2.cloned.1.call-update
  34.4 0.0 reduce-scatter.2.cloned.1.call-start
  34.5 745.5 %all-reduce.2.cloned.1.call-done = f32[1024,6144]{1,0:T(8,128)} async-done(((f32[1024,6144]{1,0:T(8,128)}), f32[1024,6144]{1,0:T(8,128)}) %all-reduce.2.cloned.1.call-update) | async-done | bytes 25165840 | tf_op jit(solution)/shard_map/psum | solution.py:36
  780.0 19.7 %fusion.6 = bf16[1024,6144]{1,0:T(8,128)(2,1)S(1)} fusion(f32[1024,6144]{1,0:T(8,128)} %all-reduce.2.cloned.1.call-done, bf16[1024,6144]{1,0:T(8,128)(2,1)} %param.6), kind=kLoop, calls=%fused_computation.15 | loop fusion | flops 125829120 | bytes 50331648 | tf_op jit(solution)/shard_map/convert_element_type | solution.py:37
  799.8 0.0 copy-start.1
  799.8 4.8 copy-done.1
  804.5 24.3 %fusion.22 = f32[1024,1536]{1,0:T(8,128)} fusion(bf16[1024,6144]{1,0:T(8,128)(2,1)S(1)} %fusion.6, bf16[1536,6144]{1,0:T(8,128)(2,1)} %param.8), kind=kOutput, calls=%fused_computation.30 | convolution fusion | flops 19327352832 | bytes 37748736 | tf_op jit(solution)/shard_map/dot_general | solution.py:41
  828.8 0.0 reduce-scatter.2.cloned.1.call-update
  828.9 0.0 copy-start.2
  828.9 31.3 %multiply_convert_fusion = bf16[6144,1536]{1,0:T(8,128)(2,1)} fusion(bf16[1024,1536]{1,0:T(8,128)(2,1)S(1)} %copy-done, bf16[1024,6144]{1,0:T(8,128)(2,1)} %param.6), kind=kOutput, calls=%fused_computation.7 | convolution fusion | flops 19409141760 | bytes 34603008 | tf_op jit(solution)/shard_map/dot_general | solution.py:31
  860.2 0.0 copy-done.2
  860.2 28.7 %fusion.11 = bf16[1536,6144]{0,1:T(8,128)(2,1)} fusion(bf16[1024,6144]{1,0:T(8,128)(2,1)} %copy-done.1, bf16[1024,1536]{1,0:T(8,128)(2,1)S(1)} %copy-done.2), kind=kOutput, calls=%fused_computation.20 | convolution fusion | flops 19346227200 | bytes 34603008 | tf_op jit(solution)/shard_map/dot_general | solution.py:38
  888.8 24.6 %copy.8 = bf16[1536,6144]{1,0:T(8,128)(2,1)} copy(bf16[1536,6144]{0,1:T(8,128)(2,1)} %fusion.11) | data formatting | bytes 37748736
  913.4 0.0 reduce-scatter.2.cloned.1.call-done
  913.4 2.4 convert_element_type.23
Async XLA Ops:
  7.2 1.9 copy-start
  7.2 772.8 %all-reduce.2.cloned.1.call-start = ((), (), s32[]{:S(2)}) async-start(), calls=%async_computation.1 | async-start | bytes 50331648 | tf_op jit(solution)/shard_map/psum | solution.py:36
  34.4 879.0 %reduce-scatter.2.cloned.1.call-start = ((), (), s32[]{:S(2)}) async-start(), calls=%async_computation.2 | async-start | bytes 7864320 | tf_op jit(solution)/shard_map/reduce_scatter | solution.py:45
  799.8 4.8 copy-start.1
  828.9 31.3 %copy-start.2 = (bf16[1024,1536]{1,0:T(8,128)(2,1)S(1)}, bf16[1024,1536]{1,0:T(8,128)(2,1)}, u32[]{:S(2)}) copy-start(bf16[1024,1536]{1,0:T(8,128)(2,1)} %param.5) | copy-start | bytes 9437188
Sparse Core Ops, SparseCore 0:
  34.6 745.4 all-reduce.1
  829.0 57.9 reduce-scatter.1
where the time goes:
time: 923 us
  waiting for transfers between devices  746 us (81%)
  matrix products  110 us (12%)
  local copies, waits for them, and re-layouts  31.2 us (3%)
  other arithmetic  22.1 us (2%)
  between operations  14.1 us (2%)
    psum x1, waiting for transfers between devices, body(): summed = lax.psum(local_sum, 'row')  746 us
    dot_general x1, matrix products, body(): lax.dot_general(activated, out_grad, CONTRACT_FIRST, preferred_element_ty...  31.3 us
    unnamed x7, local copies, waits for them, and re-layouts  31.2 us
    dot_general x1, matrix products, body(): lax.dot_general(layer_input, hidden_grad, CONTRACT_FIRST, preferred_eleme...  28.7 us
    dot_general x1, matrix products, body(): lax.dot_general(out_grad, w_down, CONTRACT_LAST, preferred_element_type=j...  25.3 us
    dot_general x1, matrix products, body(): lax.dot_general(hidden_grad, w_up, CONTRACT_LAST, preferred_element_type=...  24.3 us
    convert_element_type x1, other arithmetic, body(): hidden_grad = (summed * gelu_slope(pre_act)).astype(jnp.bfloat16)  19.7 us
  transfers between devices with their start and end apart: 2, of which 1 were waited for; matrix products, arithmetic and copies ran while one was open for 9% of the time, Pallas kernels for 0%

commit v1 on v0

--- a/solution.py
+++ b/solution.py
@@ -33,7 +33,7 @@
     )
     down_grad = (down_total * scaling).astype(jnp.bfloat16)
     local_sum = lax.dot_general(out_grad, w_down, CONTRACT_LAST, preferred_element_type=jnp.float32)
-    summed = lax.psum(local_sum, "row")
+    summed = jnp.sum(lax.all_gather(local_sum, "row"), axis=0)
     hidden_grad = (summed * gelu_slope(pre_act)).astype(jnp.bfloat16)
     up_total = lax.dot_general(
         layer_input, hidden_grad, CONTRACT_FIRST, preferred_element_type=jnp.float32

time: 923 us -> 4030 us (4.37)
  waiting for transfers between devices: 746 us -> 3790 us
  other arithmetic: 22.1 us -> 92.3 us
    all_gather x0 -> x1, waiting for transfers between devices: none -> 3790 us  [body(): summed = jnp.sum(lax.all_gather(local_sum, 'row'), axis=0)]
    psum x1 -> x0, waiting for transfers between devices: 746 us -> none  [body(): summed = lax.psum(local_sum, 'row')]
    reduce_sum x0 -> x1, other arithmetic: none -> 70.2 us  [body(): summed = jnp.sum(lax.all_gather(local_sum, 'row'), axis=0)]
  transfers between devices with their start and end apart: 2 -> 2, of which waited for: 1 -> 1; matrix products, arithmetic and copies ran while one was open for 9% -> 2% of each run, Pallas kernels for 0% -> 0%
where the time goes in v1:
time: 4030 us
  waiting for transfers between devices  3790 us (94%)
  matrix products  110 us (3%)
  other arithmetic  92.3 us (2%)
    all_gather x1, waiting for transfers between devices, body(): summed = jnp.sum(lax.all_gather(local_sum, 'row'), axis=0)  3790 us
  transfers between devices with their start and end apart: 2, of which 1 were waited for; matrix products, arithmetic and copies ran while one was open for 2% of the time, Pallas kernels for 0%

profile of v1, /device:TPU:0, one launch (start us, length us, event | category | flops | bytes accessed | tf_op | source)
XLA Modules:
  0.0 4033.7 jit_solution(5011617372208687561)
XLA Ops:
  7.2 0.0 copy-start
  7.2 0.0 all-gather.3.cloned.1.call-start
  7.2 1.8 copy-done
  9.1 25.3 fusion.21
  34.4 0.0 all-gather.3.cloned.1.call-update
  34.4 0.2 reduce-scatter.2.cloned.1.call-start
  34.6 3786.2 %all-gather.3.cloned.1.call-done = f32[8192,6144]{1,0:T(8,128)} async-done(((f32[1024,6144]{1,0:T(8,128)}), f32[8192,6144]{1,0:T(8,128)}) %all-gather.3.cloned.1.call-update) | async-done | bytes 201326608 | tf_op jit(solution)/shard_map/all_gather | solution.py:36
  3820.8 70.2 %reduce_sum.9 = f32[1024,6144]{1,0:T(8,128)} reduce(f32[8,1024,6144]{2,1,0:T(8,128)} %bitcast, f32[]{:T(128)} %constant.7.clone.1), dimensions={0}, to_apply=%region_0.0 | reduce | flops 44040192 | bytes 226492416 | tf_op jit(solution)/shard_map/reduce_sum | solution.py:36
  3891.0 19.7 fusion.6
  3910.7 0.0 copy-start.1
  3910.8 4.8 copy-done.1
  3915.5 24.3 fusion.22
  3939.8 0.0 reduce-scatter.2.cloned.1.call-update
  3939.8 0.0 copy-start.2
  3939.8 31.4 multiply_convert_fusion
  3971.3 0.0 copy-done.2
  3971.3 28.7 fusion.11
  3999.9 24.6 copy.8
  4024.5 0.0 reduce-scatter.2.cloned.1.call-done
  4024.5 2.4 convert_element_type.23
Async XLA Ops:
  7.2 1.9 copy-start
  7.2 3813.7 %all-gather.3.cloned.1.call-start = ((), (), s32[]{:S(2)}) async-start(), calls=%async_computation.2 | async-start | bytes 226492416 | tf_op jit(solution)/shard_map/all_gather | solution.py:36
  34.4 3990.1 %reduce-scatter.2.cloned.1.call-start = ((), (), s32[]{:S(2)}) async-start(), calls=%async_computation.1 | async-start | bytes 7864320 | tf_op jit(solution)/shard_map/reduce_scatter | solution.py:45
  3910.7 4.8 copy-start.1
  3939.8 31.4 copy-start.2
Sparse Core Ops, SparseCore 0:
  34.5 3786.2 all-gather.2
  3939.9 58.8 reduce-scatter.1
